TPU v7x, 32 devices: a whole 2x2x4 slice. The times are simulated.
32 devices in a mesh: layer: 2 (over core), feat: 4 (over y, x), seq: 4 (over z).
Axes of the slice: x: 2, y: 2, z: 4, core: 2. Of those that a mesh axis runs over, the one named last changes fastest.
Arguments:
- mlp_inputs: bfloat16 [2, 768, 2304], P('layer', 'seq'), may hold values from -6 to 6
- enc_weight: bfloat16 [2, 2304, 4096], P('layer', 'seq', 'feat'), may hold values from -0.125 to 0.125
- enc_bias: float32 [2, 4096], P('layer', 'feat'), may hold values from -3 to 3
- dec_weight: bfloat16 [2, 4096, 2304], P('layer', 'feat', 'seq'), may hold values from -0.1875 to 0.1875
- dec_cross: bfloat16 [4096, 2304], P('feat', ('layer', 'seq')), may hold values from -0.1875 to 0.1875
- dec_bias: float32 [2, 2304], P('layer', 'feat'), may hold values from -3 to 3
Outputs:
- recon: bfloat16 [2, 768, 2304], P('layer', 'seq', 'feat')
All inputs are finite; a program needn't handle non-finite values.
Results may differ from a plain program's by a relative error of at most 0.0047.
Values may be sent and summed in bfloat16 or wider, within the bound.
A program may use at most 64 MiB of HBM per device.

v0:
```python
import jax
import jax.numpy as jnp
from jax import lax
from jax.sharding import PartitionSpec as P


def passed_along(x, axis, by):
    devices = lax.axis_size(axis)
    pairs = [(i, i + by) for i in range(devices) if 0 <= i + by < devices]
    return lax.ppermute(x, axis, pairs)


def per_device(mlp_inputs, enc_weight, enc_bias, dec_weight, dec_cross, dec_bias):
    token_rows = mlp_inputs[0]
    layer_index = lax.axis_index("layer")
    pre_acts = jnp.dot(
        token_rows,
        lax.all_gather(enc_weight[0], "seq", axis=0, tiled=True),
        preferred_element_type=jnp.float32,
    )
    features = jnp.maximum(pre_acts + enc_bias[0], 0.0).astype(jnp.bfloat16)
    own_terms = jnp.dot(
        features,
        lax.all_gather(dec_weight[0], "seq", axis=1, tiled=True),
        preferred_element_type=jnp.float32,
    )
    half_rows = features.shape[0] // 2
    sent_half = passed_along(features[half_rows:], "layer", 1)
    cross_input = jnp.where(layer_index == 0, features[:half_rows], sent_half)
    cross_terms = jnp.dot(
        cross_input,
        lax.all_gather(dec_cross, ("layer", "seq"), axis=1, tiled=True),
        preferred_element_type=jnp.float32,
    )
    own_sums, cross_sums = (
        lax.psum_scatter(own_terms, "feat", scatter_dimension=1, tiled=True),
        lax.psum_scatter(cross_terms, "feat", scatter_dimension=1, tiled=True),
    )
    moved_sums = passed_along(cross_sums, "layer", 1)
    cross_full = jnp.concatenate([moved_sums, cross_sums], axis=0)
    total = own_sums + dec_bias[0] + jnp.where(layer_index == 1, cross_full, 0.0)
    return total.astype(jnp.bfloat16)[None]


def solution(mesh):
    placed = (
        P("layer", "seq", None),
        P("layer", "seq", "feat"),
        P("layer", "feat"),
        P("layer", "feat", "seq"),
        P("feat", ("layer", "seq")),
        P("layer", "feat"),
    )
    return jax.shard_map(
        per_device, mesh=mesh, in_specs=placed, out_specs=P("layer", "seq", "feat"), check_vma=False
    )
```

profile of v0, /device:TPU:29, one launch (start us, length us, event | category | flops | bytes accessed | tf_op | source)
XLA Modules:
  0.0 318.9 jit_solution(13372327382899990657)
XLA Ops:
  6.5 0.0 copy-start
  6.5 0.0 all-gather.8.cloned.1.call-start
  6.5 0.7 all-gather.8.cloned.1.call-update
  7.3 0.0 all-gather.6.cloned.1.call-start
  7.3 0.7 all-gather.6.cloned.1.call-update
  8.0 0.0 all-gather.10.cloned.1.call-start
  8.1 0.7 all-gather.10.cloned.1.call-update
  8.7 0.0 reduce-scatter.9.cloned.1.call-start
  8.8 88.0 %all-gather.8.cloned.1.call-done = bf16[1,2304,1024]{2,1,0:T(8,128)(2,1)} async-done(((bf16[1,576,1024]{2,1,0:T(8,128)(2,1)}), bf16[1,2304,1024]{2,1,0:T(8,128)(2,1)}) %all-gather.8.cloned.1.call-update) | async-done | bytes 4718608 | tf_op jit(solution)/shard_map/all_gather | solution.py:18
  96.8 0.0 copy-done
  96.8 3.4 %fusion.13 = bf16[192,1024]{1,0:T(8,128)(2,1)S(1)} fusion(bf16[1,2304,1024]{2,1,0:T(8,128)(2,1)} %all-gather.8.cloned.1.call-done, bf16[1,192,2304]{2,1,0:T(8,128)(2,1)S(1)} %copy-done, f32[1024]{0:T(1024)} %bitcast.30), kind=kOutput, calls=%fused_computation.8 | convolution fusion | flops 906559488 | bytes 6000640 | tf_op jit(solution)/shard_map/dot_general | solution.py:16
  100.3 1.3 collective-permute-start
  101.6 2.0 collective-permute-done
  103.6 45.1 %all-gather.6.cloned.1.call-done = bf16[1024,2304]{0,1:T(8,128)(2,1)} async-done(((bf16[1024,288]{0,1:T(8,128)(2,1)}), bf16[1024,2304]{0,1:T(8,128)(2,1)}) %all-gather.6.cloned.1.call-update) | async-done | bytes 4718608 | tf_op jit(solution)/shard_map/all_gather | solution.py:32
  148.7 4.8 %convolution_bitcast_fusion = f32[2304,96]{1,0:T(8,128)} fusion(bf16[1024,2304]{0,1:T(8,128)(2,1)} %all-gather.6.cloned.1.call-done, bf16[96,1024]{1,0:T(8,128)(2,1)S(1)} %collective-permute-done, bf16[192,1024]{1,0:T(8,128)(2,1)S(1)} %fusion.13, pred[]{:T(512)S(6)} %eq.7), kind=kOutput, calls=%fused_computation.5 | convolution fusion | flops 453083136 | bytes 5996545
  153.4 0.0 reduce-scatter.9.cloned.1.call-update
  153.5 0.0 copy-start.1
  153.5 0.0 reduce-scatter.7.cloned.1.call-start
  153.5 84.3 %all-gather.10.cloned.1.call-done = bf16[1,1024,2304]{1,2,0:T(8,128)(2,1)} async-done(((bf16[1,1024,576]{1,2,0:T(8,128)(2,1)}), bf16[1,1024,2304]{1,2,0:T(8,128)(2,1)}) %all-gather.10.cloned.1.call-update) | async-done | bytes 4718608 | tf_op jit(solution)/shard_map/all_gather | solution.py:24
  237.8 5.2 %fusion.4 = f32[2304,192]{1,0:T(8,128)} fusion(bf16[192,1024]{1,0:T(8,128)(2,1)S(1)} %fusion.13, bf16[1,1024,2304]{1,2,0:T(8,128)(2,1)} %all-gather.10.cloned.1.call-done), kind=kOutput, calls=%fused_computation.4 | convolution fusion | flops 905969664 | bytes 6881280
  243.0 0.0 reduce-scatter.7.cloned.1.call-update
  243.0 27.0 %reduce-scatter.9.cloned.1.call-done = f32[576,96]{1,0:T(8,128)} async-done(((f32[2304,96]{1,0:T(8,128)}), f32[576,96]{1,0:T(8,128)}) %reduce-scatter.9.cloned.1.call-update) | async-done | bytes 221200
  270.0 1.1 copy.10
  271.1 1.3 collective-permute-start.1
  272.4 0.0 copy-done.1
  272.4 37.9 %reduce-scatter.7.cloned.1.call-done = f32[576,192]{1,0:T(8,128)} async-done(((f32[2304,192]{1,0:T(8,128)}), f32[576,192]{1,0:T(8,128)}) %reduce-scatter.7.cloned.1.call-update) | async-done | bytes 442384
  310.3 1.3 copy.8
  311.6 0.0 collective-permute-done.1
  311.6 0.8 fusion.19
  (2 shorter events, 0.0 us)
Async XLA Ops:
  6.5 90.3 %copy-start = (bf16[1,192,2304]{2,1,0:T(8,128)(2,1)S(1)}, bf16[1,192,2304]{2,1,0:T(8,128)(2,1)}, u32[]{:S(2)}) copy-start(bf16[1,192,2304]{2,1,0:T(8,128)(2,1)} %param.6) | copy-start | bytes 2654212
  6.5 90.3 %all-gather.8.cloned.1.call-start = ((), (), s32[]{:S(2)}) async-start(), calls=%async_computation.3 | async-start | bytes 5898240 | tf_op jit(solution)/shard_map/all_gather | solution.py:18
  7.3 141.4 %all-gather.6.cloned.1.call-start = ((), (), s32[]{:S(2)}) async-start(), calls=%async_computation.2 | async-start | bytes 5308416 | tf_op jit(solution)/shard_map/all_gather | solution.py:32
  8.0 229.8 %all-gather.10.cloned.1.call-start = ((), (), s32[]{:S(2)}) async-start(), calls=%async_computation.4 | async-start | bytes 5898240 | tf_op jit(solution)/shard_map/all_gather | solution.py:24
  8.7 261.2 %reduce-scatter.9.cloned.1.call-start = ((), (), s32[]{:S(2)}) async-start(), calls=%async_computation.6 | async-start | bytes 1474560
  100.3 3.3 %collective-permute-start = (bf16[96,1024]{1,0:T(8,128)(2,1)S(1)}, bf16[96,1024]{1,0:T(8,128)(2,1)S(1)}, u32[]{:S(2)}, u32[]{:S(2)}) collective-permute-start(bf16[96,1024]{1,0:T(8,128)(2,1)S(1)} %slice.9), channel_id=1, source_target_pairs={{0,16},{1,17},{2,18},{3,19},{4,20},{5,21},{6,22},{7,23},{8,24},{9,... | collective-permute-start | bytes 589832 | tf_op jit(solution)/shard_map/ppermute | solution.py:10
  153.5 119.0 %copy-start.1 = (f32[1,576]{1,0:T(1,128)S(1)}, f32[1,576]{1,0:T(1,128)}, u32[]{:S(2)}) copy-start(f32[1,576]{1,0:T(1,128)} %param.11) | copy-start | bytes 6916
  153.5 156.8 %reduce-scatter.7.cloned.1.call-start = ((), (), s32[]{:S(2)}) async-start(), calls=%async_computation.5 | async-start | bytes 2949120
  271.1 40.5 %collective-permute-start.1 = (f32[96,576]{1,0:T(8,128)S(1)}, f32[96,576]{1,0:T(8,128)S(1)}, u32[]{:S(2)}, u32[]{:S(2)}) collective-permute-start(f32[96,576]{1,0:T(8,128)S(1)} %copy.10), channel_id=1, source_target_pairs={{0,16},{1,17},{2,18},{3,19},{4,20},{5,21},{6,22},{7,23},{8,24},{9,... | collective-permute-start | bytes 663560 | tf_op jit(solution)/shard_map/ppermute | solution.py:10
Sparse Core Ops, SparseCore 0:
  8.9 87.8 all-gather.7
  98.4 50.2 all-gather.5
  150.2 87.5 all-gather.9
  240.6 29.3 reduce-scatter.8
  272.9 37.3 reduce-scatter.6
where the time goes:
time: 321 us; the launch traced here: 319 us
  waiting for transfers between devices  286 us (89%)
  matrix products  13.4 us (4%)
  between operations  13.2 us (4%)
    all_gather x1, waiting for transfers between devices, per_device(): lax.all_gather(enc_weight[0], 'seq', axis=0, tiled=True)  88 us
    all_gather x1, waiting for transfers between devices, per_device(): lax.all_gather(dec_weight[0], 'seq', axis=1, tiled=True)  84.3 us
    unnamed x7, waiting for transfers between devices  67 us
    all_gather x1, waiting for transfers between devices, per_device(): lax.all_gather(dec_cross, ('layer', 'seq'), axis=1, tiled=True)  45.1 us
    unnamed x2, matrix products  9.93 us
  transfers between devices with their start and end apart: 7, of which 6 were waited for; matrix products, arithmetic and copies ran while one was open for 5% of the time, Pallas kernels for 0%

commit v1 on v0

v1 whole, which is shorter than its diff:
```python
import functools

import jax
import jax.numpy as jnp
from jax import lax
from jax.experimental import pallas as pl
from jax.experimental.pallas import tpu as pltpu
from jax.sharding import PartitionSpec as P

MESH = pl.DeviceIdType.MESH
F32, BF16 = jnp.float32, jnp.bfloat16


def passed_along(x, axis, by):
    devices = lax.axis_size(axis)
    pairs = [(i, i + by) for i in range(devices) if 0 <= i + by < devices]
    return lax.ppermute(x, axis, pairs)


def per_device(mlp_inputs, enc_weight, enc_bias, dec_weight, dec_cross, dec_bias):
    token_rows = mlp_inputs[0]
    layer_index = lax.axis_index("layer")
    pre_acts = jnp.dot(
        token_rows,
        lax.all_gather(enc_weight[0], "seq", axis=0, tiled=True),
        preferred_element_type=F32,
    )
    features = jnp.maximum(pre_acts + enc_bias[0], 0.0).astype(BF16)
    own_terms = jnp.dot(
        features,
        lax.all_gather(dec_weight[0], "seq", axis=1, tiled=True),
        preferred_element_type=F32,
    )
    half_rows = features.shape[0] // 2
    sent_half = passed_along(features[half_rows:], "layer", 1)
    cross_input = jnp.where(layer_index == 0, features[:half_rows], sent_half)
    cross_terms = jnp.dot(
        cross_input,
        lax.all_gather(dec_cross, ("layer", "seq"), axis=1, tiled=True),
        preferred_element_type=F32,
    )
    own_sums, cross_sums = (
        lax.psum_scatter(own_terms, "feat", scatter_dimension=1, tiled=True),
        lax.psum_scatter(cross_terms, "feat", scatter_dimension=1, tiled=True),
    )
    moved_sums = passed_along(cross_sums, "layer", 1)
    cross_full = jnp.concatenate([moved_sums, cross_sums], axis=0)
    total = own_sums + dec_bias[0] + jnp.where(layer_index == 1, cross_full, 0.0)
    return total.astype(BF16)[None]


def kernel(
    n, x_ref, enc_ref, encb_ref, dec_hbm, cross_hbm, decb_ref, out_ref,
    dec_ref, cross_ref, cross2_ref, xsend, xall, pf, rs_send, rs_up, rs_dn, feats,
    oown, osend, orecv, csend, crecv, rsum, ztr, crs, zcr, fin, fcr,
    ld_sem, cw_s, cw_r, x1_s, x1_r, x2_s, x2_r, rs_s, ru_r, rd_r, au_s, au_r, ad_s, ad_r,
    o_s, o_r, c_s, c_r, e_s, e_r, ec_s, ec_r, f_s, f_r, fc_s, fc_r,
):
    layer, f, z = lax.axis_index("layer"), lax.axis_index("feat"), lax.axis_index("seq")
    r = x_ref.shape[0] // n
    k = enc_ref.shape[0]
    half = cross_ref.shape[1]
    first, second = layer == 0, layer == 1
    order = list(range(1, n)) + [0]

    def peer(dx):
        return lax.rem(f + dx, n)

    def rows(t):
        return pl.ds(pl.multiple_of(t * r, r), r)

    pending = []

    def copy(src, dst, ss, rs, to):
        a, b, c = to
        return pltpu.make_async_remote_copy(
            src_ref=src, dst_ref=dst, send_sem=ss, recv_sem=rs,
            device_id={"layer": a, "feat": b, "seq": c}, device_id_type=MESH,
        )

    def send(cond, make):
        if cond is None:
            make().start()
        else:
            pl.when(cond)(lambda: make().start())
        pending.append((cond, make))

    def arrive(cond, dst, sem):
        def wait():
            copy(dst, dst, sem, sem, (layer, f, z)).wait_recv()
        if cond is None:
            wait()
        else:
            pl.when(cond)(wait)

    load_dec = pltpu.make_async_copy(dec_hbm, dec_ref, ld_sem.at[0])
    load_dec.start()
    load_cross = pltpu.make_async_copy(cross_hbm, cross_ref, ld_sem.at[1])
    load_cross.start()

    barrier = pltpu.get_barrier_semaphore()
    greeted = [(layer, f, lax.rem(z + d, n)) for d in range(1, n)]
    greeted += [(layer, peer(d), z) for d in range(1, n)]
    greeted += [(1 - layer, peer(d), z) for d in range(n)]
    for a, b, c in greeted:
        pl.semaphore_signal(
            barrier, inc=1, device_id={"layer": a, "feat": b, "seq": c}, device_id_type=MESH
        )

    for t in range(n):
        xsend[t] = x_ref[rows(f), t * k:(t + 1) * k]
    pl.semaphore_wait(barrier, len(greeted))
    for d in range(n - 1, 0, -1):
        for sign in (1, -1):
            t = z + sign * d
            send(
                (t < n) & (t >= 0),
                lambda t=t, d=d, sign=sign: copy(
                    xsend.at[t], xall.at[f, rows(z)], x1_s.at[t], x1_r.at[z], (layer, f, t)
                ),
            )
    for t in range(n):
        @pl.when(t == z)
        def _(t=t):
            for p in range(n):
                xall[p, t * r:(t + 1) * r] = x_ref[p * r:(p + 1) * r, t * k:(t + 1) * k]
    load_cross.wait()
    send(second, lambda: copy(cross_ref, cross2_ref, cw_s.at[0], cw_r.at[0], (0, f, z)))
    for d in range(1, n):
        for sign in (1, -1):
            t = z + sign * d
            ok = (t < n) & (t >= 0)

            def wait(t=t):
                arrive(None, xall.at[f, rows(t)], x1_r.at[t])
            pl.when(ok)(wait)
            for dx in range(1, n):
                send(
                    ok,
                    lambda t=t, dx=dx: copy(
                        xall.at[f, rows(t)], xall.at[f, rows(t)],
                        x2_s.at[dx, t], x2_r.at[dx, t], (layer, peer(dx), z)
                    ),
                )

    def stage_a(i):
        dx = order[i]
        p = peer(dx)
        if dx:
            for t in range(n):
                arrive(t != z, xall.at[p, rows(t)], x2_r.at[n - dx, t])
        pf[i] = jnp.dot(xall[p], enc_ref[...], preferred_element_type=F32)
        for t in range(n - 1, 0, -1):
            @pl.when(z == 0)
            def _(t=t):
                rs_send[i, t * r:(t + 1) * r] = pf[i, t * r:(t + 1) * r].astype(BF16)
            send(z == 0, lambda t=t: copy(
                rs_send.at[i, pl.ds(t * r, r)], rs_up.at[i, pl.ds(t * r, r)],
                rs_s.at[i, t], ru_r.at[i, t], (layer, f, z + 1)))
        for t in range(n - 1):
            @pl.when(z == n - 1)
            def _(t=t):
                rs_send[i, t * r:(t + 1) * r] = pf[i, t * r:(t + 1) * r].astype(BF16)
            send(z == n - 1, lambda t=t: copy(
                rs_send.at[i, pl.ds(t * r, r)], rs_dn.at[i, pl.ds(t * r, r)],
                rs_s.at[i, t], rd_r.at[i, t], (layer, f, z - 1)))

    def relay_up(i, t):
        ok = (z > 0) & (z < t)
        part = pl.ds(t * r, r)

        @pl.when(ok)
        def _():
            arrive(None, rs_up.at[i, part], ru_r.at[i, t])
            rs_send[i, part] = (pf[i, part] + rs_up[i, part].astype(F32)).astype(BF16)
        send(ok, lambda: copy(
            rs_send.at[i, part], rs_up.at[i, part], rs_s.at[i, t], ru_r.at[i, t], (layer, f, z + 1)))

    def relay_down(i, t):
        ok = (z < n - 1) & (z > t)
        part = pl.ds(t * r, r)

        @pl.when(ok)
        def _():
            arrive(None, rs_dn.at[i, part], rd_r.at[i, t])
            rs_send[i, part] = (pf[i, part] + rs_dn[i, part].astype(F32)).astype(BF16)
        send(ok, lambda: copy(
            rs_send.at[i, part], rs_dn.at[i, part], rs_s.at[i, t], rd_r.at[i, t], (layer, f, z - 1)))

    def stage_b(i):
        for s in range(n - 1):
            relay_up(i, n - 1 - s)
            relay_down(i, s)
        mine = rows(z)

        @pl.when(z > 0)
        def _():
            arrive(None, rs_up.at[i, mine], ru_r.at[i, z])
            pf[i, mine] = pf[i, mine] + rs_up[i, mine].astype(F32)

        @pl.when(z < n - 1)
        def _():
            arrive(None, rs_dn.at[i, mine], rd_r.at[i, z])
            pf[i, mine] = pf[i, mine] + rs_dn[i, mine].astype(F32)
        feats[i, mine] = jnp.maximum(pf[i, mine] + encb_ref[...], 0.0).astype(BF16)
        send(z < n - 1, lambda: copy(
            feats.at[i, mine], feats.at[i, mine], au_s.at[i, z], au_r.at[i, z], (layer, f, z + 1)))
        send(z > 0, lambda: copy(
            feats.at[i, mine], feats.at[i, mine], ad_s.at[i, z], ad_r.at[i, z], (layer, f, z - 1)))

    def stage_c(i):
        for d in range(1, n):
            for sign, ss, rr in ((-1, au_s, au_r), (1, ad_s, ad_r)):
                t = z + sign * d
                ok = (t >= 0) & (t < n)

                def wait(t=t, rr=rr):
                    arrive(None, feats.at[i, rows(t)], rr.at[i, t])
                pl.when(ok)(wait)
                further = ok & ((z < n - 1) if sign < 0 else (z > 0))
                send(further, lambda t=t, ss=ss, rr=rr, sign=sign: copy(
                    feats.at[i, rows(t)], feats.at[i, rows(t)], ss.at[i, t], rr.at[i, t],
                    (layer, f, z - sign)))

    def stage_d(i):
        dx = order[i]
        terms = jnp.dot(feats[i], dec_ref[...], preferred_element_type=F32)
        if dx:
            osend[dx] = terms.astype(BF16)
            send(None, lambda: copy(
                osend.at[dx], orecv.at[dx], o_s.at[dx], o_r.at[dx], (layer, peer(dx), z)))
        else:
            oown[...] = terms

        @pl.when(first)
        def _():
            a = jnp.dot(feats[i], cross_ref[...], preferred_element_type=F32)
            b = jnp.dot(feats[i], cross2_ref[...], preferred_element_type=F32)
            csend[dx] = jnp.concatenate([a, b], axis=1).astype(BF16)
        send(first, lambda: copy(
            csend.at[dx], crecv.at[dx], c_s.at[dx], c_r.at[dx], (1, peer(dx), z)))

    stage_a(0)
    for i in range(n):
        if i + 1 < n:
            stage_a(i + 1)
        stage_b(i)
        if i == 0:
            load_dec.wait()
            arrive(first, cross2_ref, cw_r.at[0])
        else:
            stage_c(i - 1)
            stage_d(i - 1)
    stage_c(n - 1)
    stage_d(n - 1)

    for dx in range(1, n):
        arrive(None, orecv.at[dx], o_r.at[dx])
        oown[...] += orecv[dx].astype(F32)
    for t in range(n):
        rsum[t] = oown[t * r:(t + 1) * r].astype(BF16)

    def scatter(cond, src, dst, ss, rs, t):
        send(cond, lambda: copy(src.at[t], dst.at[z], ss.at[t], rs.at[z], (layer, f, t)))

    for t in range(n):
        scatter(t != z, rsum, ztr, e_s, e_r, t)
    for dx in range(n):
        arrive(second, crecv.at[dx], c_r.at[dx])

    @pl.when(second)
    def _():
        sums = crecv[0].astype(F32)
        for dx in range(1, n):
            sums += crecv[dx].astype(F32)
        for t in range(n):
            for h in range(2):
                crs[h, t] = sums[t * r:(t + 1) * r, h * half:(h + 1) * half].astype(BF16)
    for t in range(n):
        for h in range(2):
            scatter(second & (t != z), crs.at[h], zcr.at[h], ec_s.at[h], ec_r.at[h], t)
    ztr[z] = rsum[z]

    @pl.when(second)
    def _():
        for h in range(2):
            zcr[h, z] = crs[h, z]

    for t in range(n):
        arrive(t != z, ztr.at[t], e_r.at[t])

        @pl.when(t == f)
        def _(t=t):
            fin[f] = ztr[t]
        send(t != f, lambda t=t: copy(
            ztr.at[t], fin.at[f], f_s.at[t], f_r.at[f], (layer, t, z)))
    for t in range(n):
        for h in range(2):
            arrive(second & (t != z), zcr.at[h, t], ec_r.at[h, t])
            to, j = (h * n + t) // 2, (h * n + t) % 2

            @pl.when(second & (to == f))
            def _(t=t, h=h, j=j):
                fcr[j, f] = zcr[h, t]
            send(second & (to != f), lambda t=t, h=h, to=to, j=j: copy(
                zcr.at[h, t], fcr.at[j, f], fc_s.at[h, t], fc_r.at[j, f], (layer, to, z)))
    for g in range(n):
        arrive(g != f, fin.at[g], f_r.at[g])
        for j in range(2):
            arrive(second & (g != f), fcr.at[j, g], fc_r.at[j, g])
        part = slice(g * r, (g + 1) * r)

        @pl.when(first)
        def _(g=g, part=part):
            out_ref[part] = (fin[g].astype(F32) + decb_ref[...]).astype(BF16)

        @pl.when(second)
        def _(g=g, part=part):
            cross = jnp.concatenate([fcr[0, g].astype(F32), fcr[1, g].astype(F32)], axis=1)
            out_ref[part] = (fin[g].astype(F32) + cross + decb_ref[...]).astype(BF16)

    for cond, make in pending:
        if cond is None:
            make().wait_send()
        else:
            pl.when(cond)(lambda make=make: make().wait_send())


def by_kernel(n, mlp_inputs, enc_weight, enc_bias, dec_weight, dec_cross, dec_bias):
    x, enc, dec = mlp_inputs[0], enc_weight[0], dec_weight[0]
    r = x.shape[0] // n
    k, wide = enc.shape
    cols, half = dec.shape[1], dec_cross.shape[1]
    vmem = pl.BlockSpec(memory_space=pltpu.VMEM)
    hbm = pl.BlockSpec(memory_space=pl.ANY)
    dma = pltpu.SemaphoreType.DMA
    every = n * r
    scratch = [
        pltpu.VMEM(dec.shape, BF16),
        pltpu.VMEM(dec_cross.shape, BF16),
        pltpu.VMEM(dec_cross.shape, BF16),
        pltpu.VMEM((n, r, k), BF16),
        pltpu.VMEM((n, every, k), BF16),
        pltpu.VMEM((n, every, wide), F32),
        pltpu.VMEM((n, every, wide), BF16),
        pltpu.VMEM((n, every, wide), BF16),
        pltpu.VMEM((n, every, wide), BF16),
        pltpu.VMEM((n, every, wide), BF16),
        pltpu.VMEM((every, cols), F32),
        pltpu.VMEM((n, every, cols), BF16),
        pltpu.VMEM((n, every, cols), BF16),
        pltpu.VMEM((n, every, 2 * half), BF16),
        pltpu.VMEM((n, every, 2 * half), BF16),
        pltpu.VMEM((n, r, cols), BF16),
        pltpu.VMEM((n, r, cols), BF16),
        pltpu.VMEM((2, n, r, half), BF16),
        pltpu.VMEM((2, n, r, half), BF16),
        pltpu.VMEM((n, r, cols), BF16),
        pltpu.VMEM((2, n, r, half), BF16),
        dma((2,)), dma((1,)), dma((1,)),
        dma((n,)), dma((n,)), dma((n, n)), dma((n, n)),
        dma((n, n)), dma((n, n)), dma((n, n)),
        dma((n, n)), dma((n, n)), dma((n, n)), dma((n, n)),
        dma((n,)), dma((n,)), dma((n,)), dma((n,)),
        dma((n,)), dma((n,)), dma((2, n)), dma((2, n)),
        dma((n,)), dma((n,)), dma((2, n)), dma((2, n)),
    ]
    out = pl.pallas_call(
        functools.partial(kernel, n),
        out_shape=jax.ShapeDtypeStruct((x.shape[0], cols), BF16),
        in_specs=[vmem, vmem, vmem, hbm, hbm, vmem],
        out_specs=vmem,
        scratch_shapes=scratch,
        compiler_params=pltpu.CompilerParams(
            collective_id=0, has_side_effects=True, vmem_limit_bytes=56 * 2**20
        ),
    )(x, enc, enc_bias, dec, dec_cross, dec_bias)
    return out[None]


def solution(mesh):
    placed = (
        P("layer", "seq", None),
        P("layer", "seq", "feat"),
        P("layer", "feat"),
        P("layer", "feat", "seq"),
        P("feat", ("layer", "seq")),
        P("layer", "feat"),
    )
    groups = mesh.shape["feat"]

    def body(mlp_inputs, *rest):
        fits = groups == mesh.shape["seq"] and mlp_inputs.shape[1] % (16 * groups) == 0
        if fits and mesh.shape["layer"] == 2 and groups % 2 == 0:
            return by_kernel(groups, mlp_inputs, *rest)
        return per_device(mlp_inputs, *rest)

    return jax.shard_map(
        body, mesh=mesh, in_specs=placed, out_specs=P("layer", "seq", "feat"), check_vma=False
    )
```

time: 321 us -> 117 us (0.36)
  waiting for transfers between devices: 286 us -> 0 us
  Pallas kernels: 0 us -> 111 us
  matrix products: 13.4 us -> 0 us
  between operations: 13.2 us -> 0.01 us
    all_gather x3 -> x0, waiting for transfers between devices: 217 us -> none  [the longest x1 88 us: per_device(): lax.all_gather(enc_weight[0], 'seq', axis=0, tiled=True)]
    pallas_call x0 -> x1, Pallas kernels: none -> 111 us  [by_kernel(): pl.pallas_call(functools.partial(kernel, n), out_shape=jax.ShapeDtypeStru...]
    unnamed x7 -> x0, waiting for transfers between devices: 67 us -> none
    unnamed x2 -> x0, matrix products: 9.93 us -> none
    dot_general x1 -> x0, matrix products: 3.43 us -> none  [per_device(): jnp.dot(token_rows, lax.all_gather(enc_weight[0], 'seq', axis=0, tiled=Tr...]
  transfers between devices with their start and end apart: 7 -> 0, of which waited for: 6 -> 0; matrix products, arithmetic and copies ran while one was open for 5% -> 0% of each run, Pallas kernels for 0% -> 0%
where the time goes in v1:
time: 117 us; the launch traced here: 116 us
  Pallas kernels  111 us (95%)
  local copies, waits for them, and re-layouts  5.47 us (5%)
    pallas_call x1, Pallas kernels, by_kernel(): pl.pallas_call(functools.partial(kernel, n), out_shape=jax.ShapeDtypeStru...  111 us
    unnamed x5, local copies, waits for them, and re-layouts  5.47 us

profile of v1, /device:TPU:29, one launch (start us, length us, event | category | flops | bytes accessed | tf_op | source)
XLA Modules:
  0.0 116.4 jit_solution(17169078208636227836)
XLA Ops:
  0.0 0.0 copy-start
  0.0 2.4 %copy.8.cross_hbm = bf16[1024,288]{1,0:T(8,128)(2,1)} copy(bf16[1024,288]{0,1:T(8,128)(2,1)} %param.10) | data formatting | bytes 1179648 | tf_op args[4]
  2.4 0.0 copy-done
  2.4 1.4 %copy.7 = bf16[1,1024,576]{2,1,0:T(8,128)(2,1)} copy(bf16[1,1024,576]{1,2,0:T(8,128)(2,1)S(1)} %copy-done) | data formatting | bytes 2359296 | tf_op args[3]
  3.8 110.9 %shard_map.64 = bf16[192,576]{1,0:T(8,128)(2,1)} custom-call(bf16[192,2304]{1,0:T(8,128)(2,1)} %bitcast.7, bf16[576,1024]{1,0:T(8,128)(2,1)} %bitcast.5, f32[1,1024]{1,0:T(1,128)} %encb_ref.1, bf16[1024,576]{1,0:T(8,128)(2,1)} %bitcast.4, bf16[1024,288]{1,0:T(8,128)(2,1)} %copy.8.cross_hbm, f32[1,576]{1,0:T(1,128)} %decb_ref.1), custom_call_target="tpu_custom_call" | custom-call | tf_op jit(solution)/shard_map/pallas_call | solution.py:368
  114.7 1.7 %copy.10 = bf16[1,192,576]{2,1,0:T(8,128)(2,1)} copy(bf16[1,192,576]{2,1,0:T(8,128)(2,1)} %bitcast.6) | data formatting | bytes 442368
Async XLA Ops:
  0.0 2.4 %copy-start = (bf16[1,1024,576]{1,2,0:T(8,128)(2,1)S(1)}, bf16[1,1024,576]{1,2,0:T(8,128)(2,1)}, u32[]{:S(2)}) copy-start(bf16[1,1024,576]{1,2,0:T(8,128)(2,1)} %param.9) | copy-start | bytes 3538948

commit v2 on v1

--- a/solution.py
+++ b/solution.py
@@ -1,4 +1,5 @@
 import functools
+import heapq
 
 import jax
 import jax.numpy as jnp
@@ -47,6 +48,63 @@
     cross_full = jnp.concatenate([moved_sums, cross_sums], axis=0)
     total = own_sums + dec_bias[0] + jnp.where(layer_index == 1, cross_full, 0.0)
     return total.astype(BF16)[None]
+
+ROW_CUTS, COL_CUTS = 3, 1
+
+
+def plan_line(n, steps, per_piece, piece=2.1, lag=1.7, touch=0.1):
+    wire = piece / per_piece
+
+    def run(ahead):
+        link, free = {}, [0.0] * n
+        got, todo, heap, lists = {}, {}, [], [[] for _ in range(n)]
+        serial = [0]
+
+        def post(now, z, to, msg):
+            start = max(link.get((z, to), 0.0), now)
+            link[z, to] = start + wire
+            serial[0] += 1
+            heapq.heappush(heap, (start + wire + lag, serial[0], to, msg))
+
+        def start(now, z, s):
+            if s < steps and z in (0, n - 1):
+                lists[z].append(("init", s, 0, 0))
+                for t in range(n - 1, 0, -1) if z == 0 else range(n - 1):
+                    post(now, z, 1 if z == 0 else n - 2, ("rs", s, t, 1 if z == 0 else -1))
+
+        def finish(z, s):
+            key = (z, s // per_piece)
+            todo[key] = todo.get(key, 0) + 1
+            if todo[key] == per_piece * n:
+                lists[z].append(("piece", s // per_piece, 0, 0))
+
+        for s in range(ahead):
+            for z in (0, n - 1):
+                start(0.0, z, s)
+        while heap:
+            now, _, z, (kind, s, t, way) = heapq.heappop(heap)
+            now = max(now, free[z]) + touch
+            free[z] = now
+            if kind == "rs" and t != z:
+                lists[z].append(("relay", s, t, way))
+                post(now, z, z + way, (kind, s, t, way))
+            elif kind == "rs":
+                got[z, s] = got.get((z, s), 0) + 1
+                if got[z, s] == (z > 0) + (z < n - 1):
+                    lists[z].append(("own", s, 0, 0))
+                    for to in (z + 1, z - 1):
+                        if 0 <= to < n:
+                            post(now, z, to, ("ag", s, z, to - z))
+                    start(now, z, s + ahead)
+                    finish(z, s)
+            else:
+                lists[z].append(("ag", s, t, way))
+                if 0 <= z + way < n:
+                    post(now, z, z + way, (kind, s, t, way))
+                finish(z, s)
+        return max(free), ahead, lists
+
+    return min(run(ahead) for ahead in range(1, steps + 1))
 
 
 def kernel(
@@ -143,6 +201,65 @@
                     ),
                 )
 
+    per_piece = ROW_CUTS * COL_CUTS
+    steps = n * per_piece
+    ru, wide = r // ROW_CUTS, enc_ref.shape[1] // COL_CUTS
+    _, ahead, lists = plan_line(n, steps, per_piece)
+
+    def where(s, t):
+        i, rest = s // per_piece, s % per_piece
+        u, c = rest // COL_CUTS, rest % COL_CUTS
+        return i, slice(t * r + u * ru, t * r + (u + 1) * ru), slice(c * wide, (c + 1) * wide)
+
+    def view(ref, s, t):
+        i, part, cols = where(s, t)
+        return ref.at[i, pl.ds(part.start, ru), pl.ds(cols.start, wide)]
+
+    later = {}
+
+    def go(zz, make):
+        make().start()
+        later.setdefault(zz, []).append(make)
+
+    def pass_sum(zz, s, t, way):
+        buf, sem = (rs_up, ru_r) if way > 0 else (rs_dn, rd_r)
+        go(zz, lambda: copy(
+            view(rs_send, s, t), view(buf, s, t), rs_s.at[s, t], sem.at[s, t], (layer, f, zz + way)))
+
+    def pass_features(zz, s, t, way):
+        ss, rr = (au_s, au_r) if way > 0 else (ad_s, ad_r)
+        go(zz, lambda: copy(
+            view(feats, s, t), view(feats, s, t), ss.at[s, t], rr.at[s, t], (layer, f, zz + way)))
+
+    def handle(zz, event):
+        kind, s, t, way = event
+        if kind == "init":
+            for t in range(n - 1, 0, -1) if zz == 0 else range(n - 1):
+                pass_sum(zz, s, t, 1 if zz == 0 else -1)
+        elif kind == "relay":
+            buf, sem = (rs_up, ru_r) if way > 0 else (rs_dn, rd_r)
+            arrive(None, view(buf, s, t), sem.at[s, t])
+            at = where(s, t)
+            rs_send[at] = (pf[at] + buf[at].astype(F32)).astype(BF16)
+            pass_sum(zz, s, t, way)
+        elif kind == "own":
+            at = where(s, zz)
+            total = pf[at] + encb_ref[:, at[2]]
+            if zz > 0:
+                arrive(None, view(rs_up, s, zz), ru_r.at[s, zz])
+                total += rs_up[at].astype(F32)
+            if zz < n - 1:
+                arrive(None, view(rs_dn, s, zz), rd_r.at[s, zz])
+                total += rs_dn[at].astype(F32)
+            feats[at] = jnp.maximum(total, 0.0).astype(BF16)
+            for way in (1, -1):
+                if 0 <= zz + way < n:
+                    pass_features(zz, s, zz, way)
+        else:
+            arrive(None, view(feats, s, t), (au_r if way > 0 else ad_r).at[s, t])
+            if 0 <= zz + way < n:
+                pass_features(zz, s, t, way)
+
     def stage_a(i):
         dx = order[i]
         p = peer(dx)
@@ -150,77 +267,10 @@
             for t in range(n):
                 arrive(t != z, xall.at[p, rows(t)], x2_r.at[n - dx, t])
         pf[i] = jnp.dot(xall[p], enc_ref[...], preferred_element_type=F32)
-        for t in range(n - 1, 0, -1):
-            @pl.when(z == 0)
-            def _(t=t):
-                rs_send[i, t * r:(t + 1) * r] = pf[i, t * r:(t + 1) * r].astype(BF16)
-            send(z == 0, lambda t=t: copy(
-                rs_send.at[i, pl.ds(t * r, r)], rs_up.at[i, pl.ds(t * r, r)],
-                rs_s.at[i, t], ru_r.at[i, t], (layer, f, z + 1)))
-        for t in range(n - 1):
-            @pl.when(z == n - 1)
-            def _(t=t):
-                rs_send[i, t * r:(t + 1) * r] = pf[i, t * r:(t + 1) * r].astype(BF16)
-            send(z == n - 1, lambda t=t: copy(
-                rs_send.at[i, pl.ds(t * r, r)], rs_dn.at[i, pl.ds(t * r, r)],
-                rs_s.at[i, t], rd_r.at[i, t], (layer, f, z - 1)))
-
-    def relay_up(i, t):
-        ok = (z > 0) & (z < t)
-        part = pl.ds(t * r, r)
-
-        @pl.when(ok)
+
+        @pl.when((z == 0) | (z == n - 1))
         def _():
-            arrive(None, rs_up.at[i, part], ru_r.at[i, t])
-            rs_send[i, part] = (pf[i, part] + rs_up[i, part].astype(F32)).astype(BF16)
-        send(ok, lambda: copy(
-            rs_send.at[i, part], rs_up.at[i, part], rs_s.at[i, t], ru_r.at[i, t], (layer, f, z + 1)))
-
-    def relay_down(i, t):
-        ok = (z < n - 1) & (z > t)
-        part = pl.ds(t * r, r)
-
-        @pl.when(ok)
-        def _():
-            arrive(None, rs_dn.at[i, part], rd_r.at[i, t])
-            rs_send[i, part] = (pf[i, part] + rs_dn[i, part].astype(F32)).astype(BF16)
-        send(ok, lambda: copy(
-            rs_send.at[i, part], rs_dn.at[i, part], rs_s.at[i, t], rd_r.at[i, t], (layer, f, z - 1)))
-
-    def stage_b(i):
-        for s in range(n - 1):
-            relay_up(i, n - 1 - s)
-            relay_down(i, s)
-        mine = rows(z)
-
-        @pl.when(z > 0)
-        def _():
-            arrive(None, rs_up.at[i, mine], ru_r.at[i, z])
-            pf[i, mine] = pf[i, mine] + rs_up[i, mine].astype(F32)
-
-        @pl.when(z < n - 1)
-        def _():
-            arrive(None, rs_dn.at[i, mine], rd_r.at[i, z])
-            pf[i, mine] = pf[i, mine] + rs_dn[i, mine].astype(F32)
-        feats[i, mine] = jnp.maximum(pf[i, mine] + encb_ref[...], 0.0).astype(BF16)
-        send(z < n - 1, lambda: copy(
-            feats.at[i, mine], feats.at[i, mine], au_s.at[i, z], au_r.at[i, z], (layer, f, z + 1)))
-        send(z > 0, lambda: copy(
-            feats.at[i, mine], feats.at[i, mine], ad_s.at[i, z], ad_r.at[i, z], (layer, f, z - 1)))
-
-    def stage_c(i):
-        for d in range(1, n):
-            for sign, ss, rr in ((-1, au_s, au_r), (1, ad_s, ad_r)):
-                t = z + sign * d
-                ok = (t >= 0) & (t < n)
-
-                def wait(t=t, rr=rr):
-                    arrive(None, feats.at[i, rows(t)], rr.at[i, t])
-                pl.when(ok)(wait)
-                further = ok & ((z < n - 1) if sign < 0 else (z > 0))
-                send(further, lambda t=t, ss=ss, rr=rr, sign=sign: copy(
-                    feats.at[i, rows(t)], feats.at[i, rows(t)], ss.at[i, t], rr.at[i, t],
-                    (layer, f, z - sign)))
+            rs_send[i] = pf[i].astype(BF16)
 
     def stage_d(i):
         dx = order[i]
@@ -241,18 +291,32 @@
             csend.at[dx], crecv.at[dx], c_s.at[dx], c_r.at[dx], (1, peer(dx), z)))
 
     stage_a(0)
+    early = min(ahead, per_piece)
+    for zz in (0, n - 1):
+        @pl.when(z == zz)
+        def _(zz=zz):
+            for s in range(early):
+                handle(zz, ("init", s, 0, 0))
+    for i in range(1, n):
+        stage_a(i)
+    load_dec.wait()
+    arrive(first, cross2_ref, cw_r.at[0])
+    segments = []
+    for zz in range(n):
+        parts = [[]]
+        for event in lists[zz]:
+            if event[0] == "piece":
+                parts.append([])
+            elif event[0] != "init" or event[1] >= early:
+                parts[-1].append(event)
+        segments.append(parts)
     for i in range(n):
-        if i + 1 < n:
-            stage_a(i + 1)
-        stage_b(i)
-        if i == 0:
-            load_dec.wait()
-            arrive(first, cross2_ref, cw_r.at[0])
-        else:
-            stage_c(i - 1)
-            stage_d(i - 1)
-    stage_c(n - 1)
-    stage_d(n - 1)
+        for zz in range(n):
+            @pl.when(z == zz)
+            def _(zz=zz, i=i):
+                for event in segments[zz][i]:
+                    handle(zz, event)
+        stage_d(i)
 
     for dx in range(1, n):
         arrive(None, orecv.at[dx], o_r.at[dx])
@@ -319,6 +383,11 @@
             cross = jnp.concatenate([fcr[0, g].astype(F32), fcr[1, g].astype(F32)], axis=1)
             out_ref[part] = (fin[g].astype(F32) + cross + decb_ref[...]).astype(BF16)
 
+    for zz in range(n):
+        @pl.when(z == zz)
+        def _(zz=zz):
+            for make in later[zz]:
+                make().wait_send()
     for cond, make in pending:
         if cond is None:
             make().wait_send()
@@ -334,7 +403,7 @@
     vmem = pl.BlockSpec(memory_space=pltpu.VMEM)
     hbm = pl.BlockSpec(memory_space=pl.ANY)
     dma = pltpu.SemaphoreType.DMA
-    every = n * r
+    every, steps = n * r, n * ROW_CUTS * COL_CUTS
     scratch = [
         pltpu.VMEM(dec.shape, BF16),
         pltpu.VMEM(dec_cross.shape, BF16),
@@ -359,8 +428,8 @@
         pltpu.VMEM((2, n, r, half), BF16),
         dma((2,)), dma((1,)), dma((1,)),
         dma((n,)), dma((n,)), dma((n, n)), dma((n, n)),
-        dma((n, n)), dma((n, n)), dma((n, n)),
-        dma((n, n)), dma((n, n)), dma((n, n)), dma((n, n)),
+        dma((steps, n)), dma((steps, n)), dma((steps, n)),
+        dma((steps, n)), dma((steps, n)), dma((steps, n)), dma((steps, n)),
         dma((n,)), dma((n,)), dma((n,)), dma((n,)),
         dma((n,)), dma((n,)), dma((2, n)), dma((2, n)),
         dma((n,)), dma((n,)), dma((2, n)), dma((2, n)),
@@ -390,7 +459,7 @@
     groups = mesh.shape["feat"]
 
     def body(mlp_inputs, *rest):
-        fits = groups == mesh.shape["seq"] and mlp_inputs.shape[1] % (16 * groups) == 0
+        fits = groups == mesh.shape["seq"] and mlp_inputs.shape[1] % (16 * ROW_CUTS * groups) == 0
         if fits and mesh.shape["layer"] == 2 and groups % 2 == 0:
             return by_kernel(groups, mlp_inputs, *rest)
         return per_device(mlp_inputs, *rest)

time: 117 us -> 94.8 us (0.81)
  Pallas kernels: 111 us -> 89.1 us
    pallas_call x1, Pallas kernels: 111 us -> 89.1 us  [by_kernel(): pl.pallas_call(functools.partial(kernel, n), out_shape=jax.ShapeDtypeStru...]
where the time goes in v2:
time: 94.8 us; the launch traced here: 94.6 us
  Pallas kernels  89.1 us (94%)
  local copies, waits for them, and re-layouts  5.47 us (6%)
    pallas_call x1, Pallas kernels, by_kernel(): pl.pallas_call(functools.partial(kernel, n), out_shape=jax.ShapeDtypeStru...  89.1 us
    unnamed x5, local copies, waits for them, and re-layouts  5.47 us

profile of v2, /device:TPU:29, one launch (start us, length us, event | category | flops | bytes accessed | tf_op | source)
XLA Modules:
  0.0 94.6 jit_solution(9954765404241640494)
XLA Ops:
  0.0 0.0 copy-start
  0.0 2.4 %copy.8.cross_hbm = bf16[1024,288]{1,0:T(8,128)(2,1)} copy(bf16[1024,288]{0,1:T(8,128)(2,1)} %param.10) | data formatting | bytes 1179648 | tf_op args[4]
  2.4 0.0 copy-done
  2.4 1.4 %copy.7 = bf16[1,1024,576]{2,1,0:T(8,128)(2,1)} copy(bf16[1,1024,576]{1,2,0:T(8,128)(2,1)S(1)} %copy-done) | data formatting | bytes 2359296 | tf_op args[3]
  3.8 89.1 %shard_map.64 = bf16[192,576]{1,0:T(8,128)(2,1)} custom-call(bf16[192,2304]{1,0:T(8,128)(2,1)} %bitcast.7, bf16[576,1024]{1,0:T(8,128)(2,1)} %bitcast.5, f32[1,1024]{1,0:T(1,128)} %encb_ref.1, bf16[1024,576]{1,0:T(8,128)(2,1)} %bitcast.4, bf16[1024,288]{1,0:T(8,128)(2,1)} %copy.8.cross_hbm, f32[1,576]{1,0:T(1,128)} %decb_ref.1), custom_call_target="tpu_custom_call" | custom-call | tf_op jit(solution)/shard_map/pallas_call | solution.py:437
  92.9 1.7 %copy.10 = bf16[1,192,576]{2,1,0:T(8,128)(2,1)} copy(bf16[1,192,576]{2,1,0:T(8,128)(2,1)} %bitcast.6) | data formatting | bytes 442368
Async XLA Ops:
  0.0 2.4 %copy-start = (bf16[1,1024,576]{1,2,0:T(8,128)(2,1)S(1)}, bf16[1,1024,576]{1,2,0:T(8,128)(2,1)}, u32[]{:S(2)}) copy-start(bf16[1,1024,576]{1,2,0:T(8,128)(2,1)} %param.9) | copy-start | bytes 3538948

commit v3 on v2

--- a/solution.py
+++ b/solution.py
@@ -50,6 +50,10 @@
     return total.astype(BF16)[None]
 
 ROW_CUTS, COL_CUTS = 3, 1
+
+
+def decoded(features, columns):
+    return lax.dot_general(features, columns, (((1,), (1,)), ((), ())), preferred_element_type=F32)
 
 
 def plan_line(n, steps, per_piece, piece=2.1, lag=1.7, touch=0.1):
@@ -109,7 +113,7 @@
 
 def kernel(
     n, x_ref, enc_ref, encb_ref, dec_hbm, cross_hbm, decb_ref, out_ref,
-    dec_ref, cross_ref, cross2_ref, xsend, xall, pf, rs_send, rs_up, rs_dn, feats,
+    dec_ref, cross_ref, xsend, xall, pf, rs_send, rs_up, rs_dn, feats,
     oown, osend, orecv, csend, crecv, rsum, ztr, crs, zcr, fin, fcr,
     ld_sem, cw_s, cw_r, x1_s, x1_r, x2_s, x2_r, rs_s, ru_r, rd_r, au_s, au_r, ad_s, ad_r,
     o_s, o_r, c_s, c_r, e_s, e_r, ec_s, ec_r, f_s, f_r, fc_s, fc_r,
@@ -117,7 +121,8 @@
     layer, f, z = lax.axis_index("layer"), lax.axis_index("feat"), lax.axis_index("seq")
     r = x_ref.shape[0] // n
     k = enc_ref.shape[0]
-    half = cross_ref.shape[1]
+    half = cross_hbm.shape[0]
+    near, far = pl.ds(0, half), pl.ds(half, half)
     first, second = layer == 0, layer == 1
     order = list(range(1, n)) + [0]
 
@@ -153,7 +158,7 @@
 
     load_dec = pltpu.make_async_copy(dec_hbm, dec_ref, ld_sem.at[0])
     load_dec.start()
-    load_cross = pltpu.make_async_copy(cross_hbm, cross_ref, ld_sem.at[1])
+    load_cross = pltpu.make_async_copy(cross_hbm, cross_ref.at[near], ld_sem.at[1])
     load_cross.start()
 
     barrier = pltpu.get_barrier_semaphore()
@@ -183,7 +188,13 @@
             for p in range(n):
                 xall[p, t * r:(t + 1) * r] = x_ref[p * r:(p + 1) * r, t * k:(t + 1) * k]
     load_cross.wait()
-    send(second, lambda: copy(cross_ref, cross2_ref, cw_s.at[0], cw_r.at[0], (0, f, z)))
+    send(second, lambda: copy(
+        cross_ref.at[near], cross_ref.at[far], cw_s.at[0], cw_r.at[0], (0, f, z)))
+    def forward(dx, t, ok):
+        send(ok, lambda: copy(
+            xall.at[f, rows(t)], xall.at[f, rows(t)],
+            x2_s.at[dx, t], x2_r.at[dx, t], (layer, peer(dx), z)))
+
     for d in range(1, n):
         for sign in (1, -1):
             t = z + sign * d
@@ -192,14 +203,10 @@
             def wait(t=t):
                 arrive(None, xall.at[f, rows(t)], x1_r.at[t])
             pl.when(ok)(wait)
-            for dx in range(1, n):
-                send(
-                    ok,
-                    lambda t=t, dx=dx: copy(
-                        xall.at[f, rows(t)], xall.at[f, rows(t)],
-                        x2_s.at[dx, t], x2_r.at[dx, t], (layer, peer(dx), z)
-                    ),
-                )
+            forward(n - 1, t, ok)
+    for dx in range(n - 2, 0, -1):
+        for t in range(n):
+            forward(dx, t, t != z)
 
     per_piece = ROW_CUTS * COL_CUTS
     steps = n * per_piece
@@ -274,7 +281,7 @@
 
     def stage_d(i):
         dx = order[i]
-        terms = jnp.dot(feats[i], dec_ref[...], preferred_element_type=F32)
+        terms = decoded(feats[i], dec_ref[...])
         if dx:
             osend[dx] = terms.astype(BF16)
             send(None, lambda: copy(
@@ -284,9 +291,7 @@
 
         @pl.when(first)
         def _():
-            a = jnp.dot(feats[i], cross_ref[...], preferred_element_type=F32)
-            b = jnp.dot(feats[i], cross2_ref[...], preferred_element_type=F32)
-            csend[dx] = jnp.concatenate([a, b], axis=1).astype(BF16)
+            csend[dx] = decoded(feats[i], cross_ref[...]).astype(BF16)
         send(first, lambda: copy(
             csend.at[dx], crecv.at[dx], c_s.at[dx], c_r.at[dx], (1, peer(dx), z)))
 
@@ -300,7 +305,7 @@
     for i in range(1, n):
         stage_a(i)
     load_dec.wait()
-    arrive(first, cross2_ref, cw_r.at[0])
+    arrive(first, cross_ref.at[far], cw_r.at[0])
     segments = []
     for zz in range(n):
         parts = [[]]
@@ -396,18 +401,17 @@
 
 
 def by_kernel(n, mlp_inputs, enc_weight, enc_bias, dec_weight, dec_cross, dec_bias):
-    x, enc, dec = mlp_inputs[0], enc_weight[0], dec_weight[0]
+    x, enc, dec, cross = mlp_inputs[0], enc_weight[0], dec_weight[0].T, dec_cross.T
     r = x.shape[0] // n
     k, wide = enc.shape
-    cols, half = dec.shape[1], dec_cross.shape[1]
+    cols, half = dec.shape[0], cross.shape[0]
     vmem = pl.BlockSpec(memory_space=pltpu.VMEM)
     hbm = pl.BlockSpec(memory_space=pl.ANY)
     dma = pltpu.SemaphoreType.DMA
     every, steps = n * r, n * ROW_CUTS * COL_CUTS
     scratch = [
         pltpu.VMEM(dec.shape, BF16),
-        pltpu.VMEM(dec_cross.shape, BF16),
-        pltpu.VMEM(dec_cross.shape, BF16),
+        pltpu.VMEM((2 * half, cross.shape[1]), BF16),
         pltpu.VMEM((n, r, k), BF16),
         pltpu.VMEM((n, every, k), BF16),
         pltpu.VMEM((n, every, wide), F32),
@@ -443,7 +447,7 @@
         compiler_params=pltpu.CompilerParams(
             collective_id=0, has_side_effects=True, vmem_limit_bytes=56 * 2**20
         ),
-    )(x, enc, enc_bias, dec, dec_cross, dec_bias)
+    )(x, enc, enc_bias, dec, cross, dec_bias)
     return out[None]
 
 

time: 94.8 us -> 89.6 us (0.945)
  local copies, waits for them, and re-layouts: 5.47 us -> 1.66 us
  Pallas kernels: 89.1 us -> 87.7 us
    unnamed x5 -> x1, local copies, waits for them, and re-layouts: 5.47 us -> 1.66 us
    pallas_call x1, Pallas kernels: 89.1 us -> 87.7 us  [by_kernel(): pl.pallas_call(functools.partial(kernel, n), out_shape=jax.ShapeDtypeStru...]
where the time goes in v3:
time: 89.6 us; the launch traced here: 89.4 us
  Pallas kernels  87.7 us (98%)
  local copies, waits for them, and re-layouts  1.66 us (2%)
    pallas_call x1, Pallas kernels, by_kernel(): pl.pallas_call(functools.partial(kernel, n), out_shape=jax.ShapeDtypeStru...  87.7 us

profile of v3, /device:TPU:29, one launch (start us, length us, event | category | flops | bytes accessed | tf_op | source)
XLA Modules:
  0.0 89.4 jit_solution(11564150092744456346)
XLA Ops:
  0.0 87.7 %shard_map.64 = bf16[192,576]{1,0:T(8,128)(2,1)} custom-call(bf16[192,2304]{1,0:T(8,128)(2,1)} %bitcast.10, bf16[576,1024]{1,0:T(8,128)(2,1)} %bitcast.7, f32[1,1024]{1,0:T(1,128)} %encb_ref.1, bf16[576,1024]{1,0:T(8,128)(2,1)} %bitcast.8, bf16[288,1024]{1,0:T(8,128)(2,1)} %bitcast.11, f32[1,576]{1,0:T(1,128)} %decb_ref.1), custom_call_target="tpu_custom_call" | custom-call | tf_op jit(solution)/shard_map/pallas_call | solution.py:441
  87.7 1.7 %copy.8 = bf16[1,192,576]{2,1,0:T(8,128)(2,1)} copy(bf16[1,192,576]{2,1,0:T(8,128)(2,1)} %bitcast.9) | data formatting | bytes 442368

commit v4 on v3

--- a/solution.py
+++ b/solution.py
@@ -267,6 +267,14 @@
             if 0 <= zz + way < n:
                 pass_features(zz, s, t, way)
 
+    def lines(events):
+        for zz in range(n):
+            if events[zz]:
+                @pl.when(z == zz)
+                def _(zz=zz):
+                    for event in events[zz]:
+                        handle(zz, event)
+
     def stage_a(i):
         dx = order[i]
         p = peer(dx)
@@ -288,6 +296,9 @@
                 osend.at[dx], orecv.at[dx], o_s.at[dx], o_r.at[dx], (layer, peer(dx), z)))
         else:
             oown[...] = terms
+
+    def stage_x(i):
+        dx = order[i]
 
         @pl.when(first)
         def _():
@@ -316,12 +327,14 @@
                 parts[-1].append(event)
         segments.append(parts)
     for i in range(n):
-        for zz in range(n):
-            @pl.when(z == zz)
-            def _(zz=zz, i=i):
-                for event in segments[zz][i]:
-                    handle(zz, event)
-        stage_d(i)
+        lines([segments[zz][i][:len(segments[zz][i]) // 2 if i else 0] for zz in range(n)])
+        if i:
+            stage_x(i - 1)
+        lines([segments[zz][i][len(segments[zz][i]) // 2 if i else 0:] for zz in range(n)])
+        if i < n - 1:
+            stage_d(i)
+    stage_x(n - 1)
+    stage_d(n - 1)
 
     for dx in range(1, n):
         arrive(None, orecv.at[dx], o_r.at[dx])

time: 89.6 us -> 88.9 us (level)
  no operation moved by 1% of the time
where the time goes in v4:
time: 88.9 us; the launch traced here: 88.8 us
  Pallas kernels  87.1 us (98%)
  local copies, waits for them, and re-layouts  1.66 us (2%)
    pallas_call x1, Pallas kernels, by_kernel(): pl.pallas_call(functools.partial(kernel, n), out_shape=jax.ShapeDtypeStru...  87.1 us

profile of v4, /device:TPU:29, one launch (start us, length us, event | category | flops | bytes accessed | tf_op | source)
XLA Modules:
  0.0 88.8 jit_solution(1609090176609722970)
XLA Ops:
  0.0 87.1 %shard_map.64 = bf16[192,576]{1,0:T(8,128)(2,1)} custom-call(bf16[192,2304]{1,0:T(8,128)(2,1)} %bitcast.10, bf16[576,1024]{1,0:T(8,128)(2,1)} %bitcast.7, f32[1,1024]{1,0:T(1,128)} %encb_ref.1, bf16[576,1024]{1,0:T(8,128)(2,1)} %bitcast.8, bf16[288,1024]{1,0:T(8,128)(2,1)} %bitcast.11, f32[1,576]{1,0:T(1,128)} %decb_ref.1), custom_call_target="tpu_custom_call" | custom-call | tf_op jit(solution)/shard_map/pallas_call | solution.py:454
  87.1 1.7 %copy.8 = bf16[1,192,576]{2,1,0:T(8,128)(2,1)} copy(bf16[1,192,576]{2,1,0:T(8,128)(2,1)} %bitcast.9) | data formatting | bytes 442368
